TPU v7x, 256 devices: a whole 4x4x8 slice. The times are simulated.
256 devices in a mesh: dp: 16 (over z, core), expert: 16 (over y, x).
Axes of the slice: x: 4, y: 4, z: 8, core: 2. Of those that a mesh axis runs over, the one named last changes fastest.
Arguments:
- cotangent: bfloat16 [32768, 2048], P(('dp', 'expert')), may hold values from -6 to 6
- saved_gate_up: bfloat16 [32768, 8, 1536], P(('dp', 'expert')), may hold values from -6 to 6
- route_ids: int32 [32768, 8], P(('dp', 'expert')), may hold values from 0 to 31, all different within a row; in each aligned block of 128 rows (0 to 127, 128 to 255, ...) at most 64 rows name the same one
- route_weights: float32 [32768, 8], P(('dp', 'expert')), may hold values from 0.05 to 1
- w_down: bfloat16 [32, 768, 2048], P('expert', 'dp'), may hold values from -0.21875 to 0.21875
Outputs:
- grad_gate_up: bfloat16 [32768, 8, 1536], P(('dp', 'expert'))
- route_grad: float32 [32768, 8], P(('dp', 'expert'))
- grad_down: float32 [32, 768, 2048], P('expert', 'dp')
Inputs may be any that keep to these rules, and one draw needn't show every extreme that they name: `route_ids`: within the rows of one device (aligned blocks of 128 tokens), no expert is named by more than 64 routes, and in every draw some expert is named by exactly 64; the 8 experts of a token are distinct.
All inputs are finite; a program needn't handle non-finite values.
Results may differ from a plain program's by a relative error of at most 0.02.
Values may be sent and summed in bfloat16 or wider, within the bound.
A program may use at most 128 MiB of HBM per device.

v0:
```python
import jax
import jax.numpy as jnp
from jax import lax
from jax.sharding import PartitionSpec as P


def slot_counts(ids, experts):
    routes = ids.shape[-1]
    onehot = (ids[..., None] == jnp.arange(experts, dtype=jnp.int32)).astype(jnp.bfloat16)
    lower = (jnp.arange(routes)[:, None] > jnp.arange(routes)[None, :]).astype(jnp.bfloat16)
    before = jnp.einsum("rq,...qe->...re", lower, onehot, preferred_element_type=jnp.float32)
    return jnp.sum(before * onehot.astype(jnp.float32), axis=-1).astype(jnp.int32)


def local(cotangent, saved_gate_up, route_ids, route_weights, w_down):
    tokens, top = route_ids.shape
    width = cotangent.shape[1]
    hidden_units = saved_gate_up.shape[2] // 2
    owners = lax.axis_size("expert")
    replicas = lax.axis_size("dp")
    me = lax.axis_index("expert")
    local_experts = w_down.shape[0]
    experts = local_experts * owners
    capacity = min(tokens, 2 * tokens * top // experts)
    routes = tokens * top
    cot_group = lax.all_gather(cotangent, "expert", axis=0, tiled=True)
    ids_group = lax.all_gather(route_ids.reshape(1, routes), "expert", axis=0, tiled=True)
    full_down = lax.all_gather(w_down, "dp", axis=1, tiled=True)
    gate = saved_gate_up[:, :, :hidden_units].astype(jnp.float32)
    up = saved_gate_up[:, :, hidden_units:].astype(jnp.float32)
    sig = jax.nn.sigmoid(gate)
    act = gate * sig
    hidden = (act * up).astype(jnp.bfloat16)
    weights = route_weights[:, :, None]
    scaled = (weights * hidden.astype(jnp.float32)).astype(jnp.bfloat16)
    flat_ids = route_ids.reshape(routes)
    slot = slot_counts(flat_ids, experts)
    position = flat_ids * capacity + slot
    slot_ids = jnp.arange(experts * capacity, dtype=jnp.int32)
    match = position[None, :] == slot_ids[:, None]
    route_of_slot = jnp.sum(
        jnp.where(match, jnp.arange(routes, dtype=jnp.int32)[None, :], 0), axis=1
    )
    filled = jnp.any(match, axis=1)
    h_rows = jnp.where(
        filled[:, None],
        scaled.reshape(routes, hidden_units)[route_of_slot],
        jnp.zeros((), jnp.bfloat16),
    )
    h_send = h_rows.reshape(owners, local_experts, capacity, hidden_units)
    slot_all = slot_counts(ids_group, experts)
    mine = me * local_experts + jnp.arange(local_experts, dtype=jnp.int32)
    pos_all = ids_group * capacity + slot_all
    want = (mine[:, None] * capacity + jnp.arange(capacity, dtype=jnp.int32)[None, :]).reshape(-1)
    hit = pos_all[:, None, :] == want[None, :, None]
    token_of = jnp.sum(
        jnp.where(hit, (jnp.arange(routes, dtype=jnp.int32) // top)[None, None, :], 0), axis=2
    )
    rows = (jnp.arange(owners, dtype=jnp.int32)[:, None] * tokens + token_of).reshape(
        owners, local_experts, capacity
    )
    rows = jnp.transpose(rows, (1, 0, 2)).reshape(local_experts, owners * capacity)
    dy_recv = cot_group[rows]
    h_recv = lax.all_to_all(h_send, "expert", split_axis=0, concat_axis=2, tiled=True)[0]
    grads = jnp.einsum(
        "jsd,jfd->jsf", dy_recv, full_down, preferred_element_type=jnp.float32
    ).astype(jnp.bfloat16)
    back = lax.all_to_all(
        grads.reshape(1, local_experts, owners * capacity, hidden_units),
        "expert",
        split_axis=2,
        concat_axis=0,
        tiled=True,
    )
    parts = []
    for j in range(local_experts):
        part = jnp.einsum(
            "sf,sd->fd", h_recv[j], dy_recv[j], preferred_element_type=jnp.float32
        ).astype(jnp.bfloat16)
        parts.append(
            lax.psum_scatter(part, "dp", scatter_dimension=0, tiled=True).astype(jnp.float32)
        )
    grad_down = jnp.stack(parts)
    returned_rows = back.reshape(experts * capacity, hidden_units)[position]
    qf = returned_rows.reshape(tokens, top, hidden_units).astype(jnp.float32)
    route_grad = jnp.sum(qf * hidden.astype(jnp.float32), -1)
    d_hidden = weights * qf
    d_gate = d_hidden * up * sig * (1.0 + gate * (1.0 - sig))
    d_up = d_hidden * act
    grad_gate_up = jnp.concatenate([d_gate, d_up], -1).astype(jnp.bfloat16)
    return (grad_gate_up, route_grad, grad_down)


def solution(mesh):
    return jax.shard_map(
        local,
        mesh=mesh,
        in_specs=(
            P(("dp", "expert"), None),
            P(("dp", "expert"), None, None),
            P(("dp", "expert"), None),
            P(("dp", "expert"), None),
            P("expert", "dp", None),
        ),
        out_specs=(
            P(("dp", "expert"), None, None),
            P(("dp", "expert"), None),
            P("expert", "dp", None),
        ),
        check_vma=False,
    )
```

profile of v0, /device:TPU:2, one launch (start us, length us, event | category | flops | bytes accessed | tf_op | source)
XLA Modules:
  0.0 409.4 jit_solution(11496074652841021074)
XLA Ops:
  7.2 0.7 all-gather.4.cloned.1.call-update
  7.9 0.7 all-gather.6.cloned.1.call-update
  8.7 0.8 copy.30
  9.5 23.6 %all-gather = s32[16,1,1024]{2,1,0:T(1,128)S(1)} all-gather(s32[1,1,1024]{2,1,0:T(1,128)S(1)} %reshape.205), channel_id=1, replica_groups=mesh['dp'=16,'expert'=16] {'expert'}, dimensions={0}, use_global_device_ids=true | all-gather | bytes 69632 | tf_op jit(solution)/shard_map/all_gather | solution.py:27
  33.4 1.4 fusion.27
  34.8 1.0 select_reduce_fusion.1
  36.1 53.2 %all-gather.4.cloned.1.call-done = bf16[2048,2048]{1,0:T(8,128)(2,1)} async-done(((bf16[128,2048]{1,0:T(8,128)(2,1)}), bf16[2048,2048]{1,0:T(8,128)(2,1)}) %all-gather.4.cloned.1.call-update) | async-done | bytes 8388624 | tf_op jit(solution)/shard_map/all_gather | solution.py:26
  89.3 20.8 %gather_fusion = bf16[2048,2048]{1,0:T(8,128)(2,1)} fusion(bf16[2048,2048]{1,0:T(8,128)(2,1)} %all-gather.4.cloned.1.call-done, s32[2048]{0:T(1024)S(1)} %bitcast_clamp_fusion), kind=kCustom, calls=%fused_computation | custom fusion | bytes 16785408 | tf_op jit(solution)/shard_map/gather | solution.py:63
  110.1 26.9 %all-gather.6.cloned.1.call-done = bf16[2,768,2048]{2,1,0:T(8,128)(2,1)} async-done(((bf16[2,48,2048]{2,1,0:T(8,128)(2,1)}), bf16[2,768,2048]{2,1,0:T(8,128)(2,1)}) %all-gather.6.cloned.1.call-update) | async-done | bytes 6291472 | tf_op jit(solution)/shard_map/all_gather | solution.py:28
  136.9 11.0 %convert_bitcast_fusion = bf16[1,2,1024,768]{3,2,1,0:T(8,128)(2,1)S(1)} fusion(bf16[2,1024,2048]{2,1,0:T(8,128)(2,1)} %bitcast.55, bf16[2,768,2048]{2,1,0:T(8,128)(2,1)} %all-gather.6.cloned.1.call-done), kind=kOutput, calls=%fused_computation.38 | convolution fusion | flops 6444023808 | bytes 17825792 | tf_op jit(solution)/shard_map/jsd,jfd->jsf/dot_general | solution.py:65
  147.9 4.9 %copy.32 = bf16[1,2,1024,768]{3,1,0,2:T(2,128)(2,1)} copy(bf16[1,2,1024,768]{3,2,1,0:T(8,128)(2,1)S(1)} %convert_bitcast_fusion) | data formatting | bytes 6291456 | tf_op jit(solution)/shard_map/reshape | solution.py:69
  152.8 7.4 %all-to-all-start = ((bf16[1,2,1024,768]{3,1,0,2:T(2,128)(2,1)}), bf16[1,2,1024,768]{3,1,0,2:T(2,128)(2,1)S(1)}, u32[]{:S(2)}, u32[]{:S(2)}) async-start(bf16[1,2,1024,768]{3,1,0,2:T(2,128)(2,1)} %copy.32), calls=%async_computation | async-start | bytes 6291456 | tf_op jit(solution)/shard_map/all_to_all | solution.py:68
  160.7 0.5 fusion.31
  161.3 1.0 fusion
  162.4 0.9 select_reduce_fusion
  163.4 41.3 %all-to-all-done = bf16[1,2,1024,768]{3,1,0,2:T(2,128)(2,1)S(1)} async-done(((bf16[1,2,1024,768]{3,1,0,2:T(2,128)(2,1)}), bf16[1,2,1024,768]{3,1,0,2:T(2,128)(2,1)S(1)}, u32[]{:S(2)}, u32[]{:S(2)}) %all-to-all-start) | async-done | bytes 3145760 | tf_op jit(solution)/shard_map/all_to_all | solution.py:68
  204.7 1.7 copy-done.1
  206.3 2.5 copy.33
  208.9 5.2 %gather_fusion.1 = bf16[1024,768]{1,0:T(8,128)(2,1)} fusion(bf16[2048,768]{1,0:T(8,128)(2,1)S(1)} %bitcast.51, s32[1024]{0:T(1024)S(1)} %broadcast_clamp_fusion.1), kind=kCustom, calls=%fused_computation.1 | custom fusion | bytes 3149824 | tf_op jit(solution)/shard_map/gather | solution.py:84
  214.1 5.0 %fusion.29 = (bf16[1024,768]{1,0:T(8,128)(2,1)S(1)}, bf16[128,8,768]{2,1,0:T(8,128)(2,1)S(1)}, bf16[128,8,768]{2,1,0:T(8,128)(2,1)}, bf16[128,8,768]{2,1,0:T(8,128)(2,1)}) fusion(f32[128,8]{1,0:T(8,128)S(1)} %copy.29, bf16[128,8,1536]{2,1,0:T(8,128)(2,1)} %param.6, bf16[1024,768]{1,0:T(8,128)(2,1)} %gather_fusion.1), kind=kLoop, calls=%fused_computation.44 | loop fusion | flops 17301504 | bytes 11014144 | tf_op jit(solution)/shard_map/reshape | solution.py:47
  219.0 9.4 %gather_fusion.2 = bf16[2048,768]{1,0:T(8,128)(2,1)} fusion(bf16[1024,768]{1,0:T(8,128)(2,1)S(1)} %get-tuple-element.9, s32[2048]{0:T(1024)S(1)} %broadcast_clamp_fusion), kind=kCustom, calls=%fused_computation.2 | custom fusion | bytes 6299648 | tf_op jit(solution)/shard_map/gather | solution.py:47
  228.4 2.3 broadcast_select_fusion
  230.7 46.5 %all_to_all.30 = bf16[16,2,64,768]{3,2,1,0:T(8,128)(2,1)S(1)} all-to-all(bf16[16,2,64,768]{3,2,1,0:T(8,128)(2,1)S(1)} %broadcast_select_fusion), channel_id=1, replica_groups=mesh['dp'=16,'expert'=16] {'expert'}, dimensions={0} | all-to-all | bytes 6291456 | tf_op jit(solution)/shard_map/all_to_all | solution.py:64
  277.5 4.9 %fusion.13 = bf16[768,2048]{1,0:T(8,128)(2,1)} fusion(bf16[1024,768]{1,0:T(8,128)(2,1)S(1)} %bitcast.59, bf16[2048,2048]{1,0:T(8,128)(2,1)S(1)} %bitcast.57), kind=kOutput, calls=%fused_computation.25 | convolution fusion | flops 3222798336 | bytes 8912896 | tf_op jit(solution)/shard_map/sf,sd->fd/dot_general | solution.py:77
  282.5 7.0 %fusion.10 = bf16[768,2048]{1,0:T(8,128)(2,1)} fusion(bf16[1024,768]{1,0:T(8,128)(2,1)S(1)} %bitcast.58, bf16[2048,2048]{1,0:T(8,128)(2,1)} %gather_fusion), kind=kOutput, calls=%fused_computation.24 | convolution fusion | flops 3222798336 | bytes 8912896 | tf_op jit(solution)/shard_map/sf,sd->fd/dot_general | solution.py:77
  289.6 1.4 copy-done
  290.9 0.5 fusion.22
  291.4 0.7 copy.36
  292.1 3.8 pad_maximum_fusion
  295.9 43.3 %reduce-scatter.5.cloned.1.call-done = bf16[48,2048]{1,0:T(8,128)(2,1)} async-done(((bf16[768,2048]{1,0:T(8,128)(2,1)}), bf16[48,2048]{1,0:T(8,128)(2,1)}) %reduce-scatter.5.cloned.1.call-update) | async-done | bytes 196624 | tf_op jit(solution)/shard_map/reduce_scatter | solution.py:81
  339.2 61.7 %reduce-scatter.3.cloned.1.call-done = bf16[48,2048]{1,0:T(8,128)(2,1)} async-done(((bf16[768,2048]{1,0:T(8,128)(2,1)}), bf16[48,2048]{1,0:T(8,128)(2,1)}) %reduce-scatter.3.cloned.1.call-update) | async-done | bytes 196624 | tf_op jit(solution)/shard_map/reduce_scatter | solution.py:81
  400.9 2.0 maximum_convert_fusion
  (44 shorter events, 1.5 us)
Async XLA Ops:
  7.2 82.1 %all-gather.4.cloned.1.call-start = ((), (), s32[]{:S(2)}) async-start(), calls=%async_computation.4 | async-start | bytes 8912896 | tf_op jit(solution)/shard_map/all_gather | solution.py:26
  7.9 129.0 %all-gather.6.cloned.1.call-start = ((), (), s32[]{:S(2)}) async-start(), calls=%async_computation.5 | async-start | bytes 6684672 | tf_op jit(solution)/shard_map/all_gather | solution.py:28
  152.8 7.5 %copy-start.3 = (f32[128,8]{0,1:T(8,128)S(1)}, f32[128,8]{0,1:T(8,128)}, u32[]{:S(2)}) copy-start(f32[128,8]{0,1:T(8,128)} %param.8) | copy-start | bytes 12292
  152.8 7.7 %copy-start.2 = (s32[128,8]{0,1:T(8,128)S(1)}, s32[128,8]{0,1:T(8,128)}, u32[]{:S(2)}) copy-start(s32[128,8]{0,1:T(8,128)} %param.7) | copy-start | bytes 12292
  152.8 51.8 %all-to-all-start = ((bf16[1,2,1024,768]{3,1,0,2:T(2,128)(2,1)}), bf16[1,2,1024,768]{3,1,0,2:T(2,128)(2,1)S(1)}, u32[]{:S(2)}, u32[]{:S(2)}) async-start(bf16[1,2,1024,768]{3,1,0,2:T(2,128)(2,1)} %copy.32), calls=%async_computation | async-start | bytes 6291456 | tf_op jit(solution)/shard_map/all_to_all | solution.py:68
  160.2 179.0 %reduce-scatter.5.cloned.1.call-start = ((), (), s32[]{:S(2)}) async-start(), calls=%async_computation.7 | async-start | bytes 3342336 | tf_op jit(solution)/shard_map/reduce_scatter | solution.py:81
  204.7 1.7 copy-start.1
  228.4 49.1 %slice-start = ((s8[8388608]{0:T(1024)(128)(4,1)}), s8[4194304]{0:T(1024)(128)(4,1)S(1)}, s32[]{:S(2)}) async-start(s8[8388608]{0:T(1024)(128)(4,1)} %bitcast.56), calls=%async_computation.8 | async-start | bytes 8388608
  230.7 46.8 %slice-start.1 = ((s8[8388608]{0:T(1024)(128)(4,1)}), s8[4194304]{0:T(1024)(128)(4,1)S(1)}, s32[]{:S(2)}) async-start(s8[8388608]{0:T(1024)(128)(4,1)} %bitcast.56), calls=%async_computation.9 | async-start | bytes 8388608
  282.4 118.5 %reduce-scatter.3.cloned.1.call-start = ((), (), s32[]{:S(2)}) async-start(), calls=%async_computation.6 | async-start | bytes 3342336 | tf_op jit(solution)/shard_map/reduce_scatter | solution.py:81
  289.5 1.4 copy-start
Sparse Core Ops, SparseCore 0:
  10.4 78.7 all-gather.3
  91.1 45.7 all-gather.5
  282.6 56.6 reduce-scatter.4
  341.6 59.2 reduce-scatter.2
where the time goes:
time: 410 us; the launch traced here: 409 us
  waiting for transfers between devices  228 us (56%)
  blocking collectives  70.2 us (17%)
  local copies, waits for them, and re-layouts  48.4 us (12%)
  matrix products  24.9 us (6%)
  other arithmetic  16.6 us (4%)
  between operations  14 us (3%)
  starting transfers between devices  7.56 us (2%)
    reduce_scatter x2, waiting for transfers between devices, local(): lax.psum_scatter(part, 'dp', scatter_dimension=0, tiled=True)  105 us
    all_gather x1, waiting for transfers between devices, local(): cot_group = lax.all_gather(cotangent, 'expert', axis=0, tiled=True)  53.2 us
    all_to_all x1, blocking collectives, local(): lax.all_to_all(h_send, 'expert', split_axis=0, concat_axis=2, tiled=True)[0]  46.5 us
    all_to_all x1, waiting for transfers between devices, local(): lax.all_to_all(grads.reshape(1, local_experts, owners * capacity, hidden_...  41.3 us
    all_gather x1, waiting for transfers between devices, local(): full_down = lax.all_gather(w_down, 'dp', axis=1, tiled=True)  26.9 us
    all_gather x1, blocking collectives, local(): lax.all_gather(route_ids.reshape(1, routes), 'expert', axis=0, tiled=True)  23.6 us
    gather x1, local copies, waits for them, and re-layouts, local(): dy_recv = cot_group[rows]  20.8 us
    dot_general x2, matrix products, local(): jnp.einsum('sf,sd->fd', h_recv[j], dy_recv[j], preferred_element_type=jnp...  11.9 us
  transfers between devices with their start and end apart: 5, of which 5 were waited for; matrix products, arithmetic and copies ran while one was open for 10% of the time, Pallas kernels for 0%

commit v1 on v0

--- a/solution.py
+++ b/solution.py
@@ -23,7 +23,9 @@
     experts = local_experts * owners
     capacity = min(tokens, 2 * tokens * top // experts)
     routes = tokens * top
-    cot_group = lax.all_gather(cotangent, "expert", axis=0, tiled=True)
+    cot_group = jnp.concatenate(
+        jax.lax.all_to_all(jnp.stack([cotangent] * jax.lax.psum(1, "expert"), 0), "expert", 0, 0), 0
+    )
     ids_group = lax.all_gather(route_ids.reshape(1, routes), "expert", axis=0, tiled=True)
     full_down = lax.all_gather(w_down, "dp", axis=1, tiled=True)
     gate = saved_gate_up[:, :, :hidden_units].astype(jnp.float32)

time: 410 us -> 445 us (1.085)
  blocking collectives: 70.2 us -> 181 us
  waiting for transfers between devices: 228 us -> 142 us
  starting transfers between devices: 7.56 us -> 13.5 us
  local copies, waits for them, and re-layouts: 48.4 us -> 53.1 us
    all_gather x1, blocking collectives: 23.6 us -> 137 us  [local(): lax.all_gather(route_ids.reshape(1, routes), 'expert', axis=0, tiled=True)]
    all_gather x1 -> x0, waiting for transfers between devices: 53.2 us -> none  [local(): cot_group = lax.all_gather(cotangent, 'expert', axis=0, tiled=True)]
    all_gather x1, waiting for transfers between devices: 26.9 us -> 0.01 us  [local(): full_down = lax.all_gather(w_down, 'dp', axis=1, tiled=True)]
    all_to_all x1, waiting for transfers between devices: 41.3 us -> 31.4 us  [local(): lax.all_to_all(grads.reshape(1, local_experts, owners * capacity, hidden_...]
    all_to_all x0 -> x1, starting transfers between devices: none -> 7.61 us  [local(): jax.lax.all_to_all(jnp.stack([cotangent] * jax.lax.psum(1, 'expert'), 0),...]
    another operation x0 -> x1, local copies, waits for them, and re-layouts: none -> 5.33 us  [local(): jnp.stack([cotangent] * jax.lax.psum(1, 'expert'), 0)]
    reduce_scatter x2, waiting for transfers between devices: 105 us -> 110 us  [local(): lax.psum_scatter(part, 'dp', scatter_dimension=0, tiled=True)]
  transfers between devices with their start and end apart: 5 -> 5, of which waited for: 5 -> 3; matrix products, arithmetic and copies ran while one was open for 10% -> 10% of each run, Pallas kernels for 0% -> 0%
where the time goes in v1:
time: 445 us
  blocking collectives  181 us (41%)
  waiting for transfers between devices  142 us (32%)
  local copies, waits for them, and re-layouts  53.1 us (12%)
  matrix products  24.9 us (6%)
  other arithmetic  16.7 us (4%)
  between operations  14 us (3%)
  starting transfers between devices  13.5 us (3%)
    all_gather x1, blocking collectives, local(): lax.all_gather(route_ids.reshape(1, routes), 'expert', axis=0, tiled=True)  137 us
    reduce_scatter x2, waiting for transfers between devices, local(): lax.psum_scatter(part, 'dp', scatter_dimension=0, tiled=True)  110 us
    all_to_all x1, blocking collectives, local(): lax.all_to_all(h_send, 'expert', split_axis=0, concat_axis=2, tiled=True)[0]  44.4 us
    all_to_all x1, waiting for transfers between devices, local(): lax.all_to_all(grads.reshape(1, local_experts, owners * capacity, hidden_...  31.4 us
    gather x1, local copies, waits for them, and re-layouts, local(): dy_recv = cot_group[rows]  20.8 us
    dot_general x2, matrix products, local(): jnp.einsum('sf,sd->fd', h_recv[j], dy_recv[j], preferred_element_type=jnp...  12 us
    dot_general x1, matrix products, local(): jnp.einsum('jsd,jfd->jsf', dy_recv, full_down, preferred_element_type=jnp...  11 us
    gather x1, local copies, waits for them, and re-layouts, local(): scaled.reshape(routes, hidden_units)[route_of_slot]  9.4 us
  transfers between devices with their start and end apart: 5, of which 3 were waited for; matrix products, arithmetic and copies ran while one was open for 10% of the time, Pallas kernels for 0%

profile of v1, /device:TPU:2, one launch (start us, length us, event | category | flops | bytes accessed | tf_op | source)
XLA Modules:
  0.0 444.7 jit_solution(17293842754861907576)
XLA Ops:
  7.2 0.7 all-gather.3.cloned.1.call-update
  7.9 5.3 %stack.13 = bf16[16,128,2048]{2,1,0:T(8,128)(2,1)} broadcast(bf16[128,2048]{1,0:T(8,128)(2,1)} %param.5), dimensions={1,2} | broadcast | bytes 8912896 | tf_op jit(solution)/shard_map/stack | solution.py:27
  13.2 7.6 %all-to-all-start = ((bf16[16,128,2048]{2,1,0:T(8,128)(2,1)}), bf16[16,128,2048]{2,1,0:T(8,128)(2,1)}, u32[]{:S(2)}, u32[]{:S(2)}) async-start(bf16[16,128,2048]{2,1,0:T(8,128)(2,1)} %stack.13), calls=%async_computation | async-start | bytes 16777216 | tf_op jit(solution)/shard_map/all_to_all | solution.py:27
  21.0 136.6 %all-gather = s32[16,1,1024]{2,1,0:T(1,128)S(1)} all-gather(s32[1,1,1024]{2,1,0:T(1,128)S(1)} %reshape.211), channel_id=1, replica_groups=mesh['dp'=16,'expert'=16] {'expert'}, dimensions={0}, use_global_device_ids=true | all-gather | bytes 69632 | tf_op jit(solution)/shard_map/all_gather | solution.py:29
  157.9 1.4 fusion.27
  159.3 1.0 select_reduce_fusion.1
  160.6 20.8 %gather_fusion = bf16[2048,2048]{1,0:T(8,128)(2,1)} fusion(bf16[2048,2048]{1,0:T(8,128)(2,1)} %bitcast, s32[2048]{0:T(1024)S(1)} %bitcast_clamp_fusion), kind=kCustom, calls=%fused_computation | custom fusion | bytes 16785408 | tf_op jit(solution)/shard_map/gather | solution.py:65
  181.4 11.0 %convert_bitcast_fusion = bf16[1,2,1024,768]{3,2,1,0:T(8,128)(2,1)S(1)} fusion(bf16[2,1024,2048]{2,1,0:T(8,128)(2,1)} %bitcast.56, bf16[2,768,2048]{2,1,0:T(8,128)(2,1)} %all-gather.3.cloned.1.call-done), kind=kOutput, calls=%fused_computation.38 | convolution fusion | flops 6444023808 | bytes 17825792 | tf_op jit(solution)/shard_map/jsd,jfd->jsf/dot_general | solution.py:67
  192.4 4.9 %copy.32 = bf16[1,2,1024,768]{3,1,0,2:T(2,128)(2,1)} copy(bf16[1,2,1024,768]{3,2,1,0:T(8,128)(2,1)S(1)} %convert_bitcast_fusion) | data formatting | bytes 6291456 | tf_op jit(solution)/shard_map/reshape | solution.py:71
  197.3 5.6 %all-to-all-start.1 = ((bf16[1,2,1024,768]{3,1,0,2:T(2,128)(2,1)}), bf16[1,2,1024,768]{3,1,0,2:T(2,128)(2,1)S(1)}, u32[]{:S(2)}, u32[]{:S(2)}) async-start(bf16[1,2,1024,768]{3,1,0,2:T(2,128)(2,1)} %copy.32), calls=%async_computation.1 | async-start | bytes 6291456 | tf_op jit(solution)/shard_map/all_to_all | solution.py:70
  202.8 0.2 reduce-scatter.5.cloned.1.call-start
  203.5 0.5 fusion.31
  204.0 1.0 fusion
  205.2 0.9 select_reduce_fusion
  206.1 31.4 %all-to-all-done.1 = bf16[1,2,1024,768]{3,1,0,2:T(2,128)(2,1)S(1)} async-done(((bf16[1,2,1024,768]{3,1,0,2:T(2,128)(2,1)}), bf16[1,2,1024,768]{3,1,0,2:T(2,128)(2,1)S(1)}, u32[]{:S(2)}, u32[]{:S(2)}) %all-to-all-start.1) | async-done | bytes 3145760 | tf_op jit(solution)/shard_map/all_to_all | solution.py:70
  237.5 1.7 copy-done.1
  239.1 2.5 copy.33
  241.7 5.2 %gather_fusion.1 = bf16[1024,768]{1,0:T(8,128)(2,1)} fusion(bf16[2048,768]{1,0:T(8,128)(2,1)S(1)} %bitcast.52, s32[1024]{0:T(1024)S(1)} %broadcast_clamp_fusion.1), kind=kCustom, calls=%fused_computation.1 | custom fusion | bytes 3149824 | tf_op jit(solution)/shard_map/gather | solution.py:86
  246.9 5.0 %fusion.29 = (bf16[1024,768]{1,0:T(8,128)(2,1)S(1)}, bf16[128,8,768]{2,1,0:T(8,128)(2,1)S(1)}, bf16[128,8,768]{2,1,0:T(8,128)(2,1)}, bf16[128,8,768]{2,1,0:T(8,128)(2,1)}) fusion(f32[128,8]{1,0:T(8,128)S(1)} %copy.29, bf16[128,8,1536]{2,1,0:T(8,128)(2,1)} %param.6, bf16[1024,768]{1,0:T(8,128)(2,1)} %gather_fusion.1), kind=kLoop, calls=%fused_computation.44 | loop fusion | flops 17301504 | bytes 11014144 | tf_op jit(solution)/shard_map/reshape | solution.py:49
  251.9 9.4 %gather_fusion.2 = bf16[2048,768]{1,0:T(8,128)(2,1)} fusion(bf16[1024,768]{1,0:T(8,128)(2,1)S(1)} %get-tuple-element.9, s32[2048]{0:T(1024)S(1)} %broadcast_clamp_fusion), kind=kCustom, calls=%fused_computation.2 | custom fusion | bytes 6299648 | tf_op jit(solution)/shard_map/gather | solution.py:49
  261.3 2.3 broadcast_select_fusion
  263.5 44.4 %all_to_all.35 = bf16[16,2,64,768]{3,2,1,0:T(8,128)(2,1)S(1)} all-to-all(bf16[16,2,64,768]{3,2,1,0:T(8,128)(2,1)S(1)} %broadcast_select_fusion), channel_id=1, replica_groups=mesh['dp'=16,'expert'=16] {'expert'}, dimensions={0} | all-to-all | bytes 6291456 | tf_op jit(solution)/shard_map/all_to_all | solution.py:66
  307.9 0.2 fusion.42
  308.2 4.9 %fusion.13 = bf16[768,2048]{1,0:T(8,128)(2,1)} fusion(bf16[1024,768]{1,0:T(8,128)(2,1)S(1)} %bitcast.60, bf16[2048,2048]{1,0:T(8,128)(2,1)S(1)} %bitcast.58), kind=kOutput, calls=%fused_computation.25 | convolution fusion | flops 3222798336 | bytes 8912896 | tf_op jit(solution)/shard_map/sf,sd->fd/dot_general | solution.py:79
  313.2 7.1 %fusion.10 = bf16[768,2048]{1,0:T(8,128)(2,1)} fusion(bf16[1024,768]{1,0:T(8,128)(2,1)S(1)} %bitcast.59, bf16[2048,2048]{1,0:T(8,128)(2,1)} %gather_fusion), kind=kOutput, calls=%fused_computation.24 | convolution fusion | flops 3222798336 | bytes 8912896 | tf_op jit(solution)/shard_map/sf,sd->fd/dot_general | solution.py:79
  320.3 1.4 copy-done
  321.7 0.5 fusion.22
  322.2 0.7 copy.36
  322.8 3.9 pad_maximum_fusion
  326.7 47.4 %reduce-scatter.5.cloned.1.call-done = bf16[48,2048]{1,0:T(8,128)(2,1)} async-done(((bf16[768,2048]{1,0:T(8,128)(2,1)}), bf16[48,2048]{1,0:T(8,128)(2,1)}) %reduce-scatter.5.cloned.1.call-update) | async-done | bytes 196624 | tf_op jit(solution)/shard_map/reduce_scatter | solution.py:83
  374.1 62.1 %reduce-scatter.3.cloned.1.call-done = bf16[48,2048]{1,0:T(8,128)(2,1)} async-done(((bf16[768,2048]{1,0:T(8,128)(2,1)}), bf16[48,2048]{1,0:T(8,128)(2,1)}) %reduce-scatter.3.cloned.1.call-update) | async-done | bytes 196624 | tf_op jit(solution)/shard_map/reduce_scatter | solution.py:83
  436.2 2.0 maximum_convert_fusion
  (44 shorter events, 1.3 us)
Async XLA Ops:
  7.2 174.2 %all-gather.3.cloned.1.call-start = ((), (), s32[]{:S(2)}) async-start(), calls=%async_computation.5 | async-start | bytes 6684672 | tf_op jit(solution)/shard_map/all_gather | solution.py:30
  13.2 7.6 %copy-start.2 = (s32[128,8]{0,1:T(8,128)S(1)}, s32[128,8]{0,1:T(8,128)}, u32[]{:S(2)}) copy-start(s32[128,8]{0,1:T(8,128)} %param.7) | copy-start | bytes 12292
  13.2 147.3 %all-to-all-start = ((bf16[16,128,2048]{2,1,0:T(8,128)(2,1)}), bf16[16,128,2048]{2,1,0:T(8,128)(2,1)}, u32[]{:S(2)}, u32[]{:S(2)}) async-start(bf16[16,128,2048]{2,1,0:T(8,128)(2,1)} %stack.13), calls=%async_computation | async-start | bytes 16777216 | tf_op jit(solution)/shard_map/all_to_all | solution.py:27
  197.3 5.9 %copy-start.3 = (f32[128,8]{0,1:T(8,128)S(1)}, f32[128,8]{0,1:T(8,128)}, u32[]{:S(2)}) copy-start(f32[128,8]{0,1:T(8,128)} %param.8) | copy-start | bytes 12292
  197.3 40.2 %all-to-all-start.1 = ((bf16[1,2,1024,768]{3,1,0,2:T(2,128)(2,1)}), bf16[1,2,1024,768]{3,1,0,2:T(2,128)(2,1)S(1)}, u32[]{:S(2)}, u32[]{:S(2)}) async-start(bf16[1,2,1024,768]{3,1,0,2:T(2,128)(2,1)} %copy.32), calls=%async_computation.1 | async-start | bytes 6291456 | tf_op jit(solution)/shard_map/all_to_all | solution.py:70
  202.8 171.3 %reduce-scatter.5.cloned.1.call-start = ((), (), s32[]{:S(2)}) async-start(), calls=%async_computation.7 | async-start | bytes 3342336 | tf_op jit(solution)/shard_map/reduce_scatter | solution.py:83
  237.5 1.7 copy-start.1
  261.3 46.9 %slice-start = ((s8[8388608]{0:T(1024)(128)(4,1)}), s8[4194304]{0:T(1024)(128)(4,1)S(1)}, s32[]{:S(2)}) async-start(s8[8388608]{0:T(1024)(128)(4,1)} %bitcast.57), calls=%async_computation.8 | async-start | bytes 8388608
  263.5 44.7 %slice-start.1 = ((s8[8388608]{0:T(1024)(128)(4,1)}), s8[4194304]{0:T(1024)(128)(4,1)S(1)}, s32[]{:S(2)}) async-start(s8[8388608]{0:T(1024)(128)(4,1)} %bitcast.57), calls=%async_computation.9 | async-start | bytes 8388608
  313.2 123.0 %reduce-scatter.3.cloned.1.call-start = ((), (), s32[]{:S(2)}) async-start(), calls=%async_computation.6 | async-start | bytes 3342336 | tf_op jit(solution)/shard_map/reduce_scatter | solution.py:83
  320.3 1.4 copy-start
Sparse Core Ops, SparseCore 0:
  9.8 48.9 all-gather.2
  313.3 60.7 reduce-scatter.4
  376.7 59.4 reduce-scatter.2
